TPU v7x, 256 devices: a whole 4x4x8 slice. The times are simulated.
256 devices in a mesh: leaf: 8 (over x, core), turn: 32 (over z, y).
Axes of the slice: x: 4, y: 4, z: 8, core: 2. Of those that a mesh axis runs over, the one named last changes fastest.
Arguments:
- echoes: bfloat16 [16384, 256, 256], P(('leaf', 'turn')), may hold values from -6 to 6
- chirp: bfloat16 [2, 128], replicated, may hold values from -0.375 to 0.375
- taps: int32 [3, 2, 128, 8], replicated, may hold values from 0 to 127, as said below
- slots: int32 [8, 32], P('leaf'), may hold values from 0 to 31, each once within a row
Outputs:
- image: bfloat16 [128, 256, 256], P('leaf', 'turn')
Inputs may be any that keep to these rules, and one draw needn't show every extreme that they name: Each row of taps is 8 consecutive beam indices starting at a - 4 + s with s from -3 to 3, clipped to the beams. Each row of slots is a permutation.
All inputs are finite; a program needn't handle non-finite values.
Results may differ from a plain program's by a relative error of at most 0.008.
Values may be sent and summed in bfloat16 or wider, within the bound.
A program may use at most 128 MiB of HBM per device.

v0:
```python
import functools
import math

import jax
import jax.numpy as jnp
from jax import lax
from jax.experimental import pallas as pl
from jax.experimental.pallas import tpu as pltpu
from jax.sharding import PartitionSpec as P

WEIGHTS = (-1.0 / 32, 3.0 / 32, -7.0 / 32, 21.0 / 32, 21.0 / 32, -7.0 / 32, 3.0 / 32, -1.0 / 32)
MESH = pl.DeviceIdType.MESH

BEAMS = 128
TAPS = 8
SUBP = 64
NSUB = 32
NZ = 8
NY = 4
NLEAF = 8
TILES = NZ * NY
COLS = 512
WIDE = 2 * COLS
BY = 80
BZ = BEAMS - BY
GRAN = 16
NGRAN = 256 // GRAN

f32 = jnp.float32
bf16 = jnp.bfloat16


def cos_sin(n):
    n = n & 4095
    quad = (n + 512) >> 10
    m = (n - (quad << 10)).astype(f32) * (2.0 * math.pi / 4096)
    m2 = m * m
    s = m * (1.0 + m2 * (-1.0 / 6 + m2 * (1.0 / 120 + m2 * (-1.0 / 5040 + m2 * (1.0 / 362880)))))
    c = 1.0 + m2 * (-0.5 + m2 * (1.0 / 24 + m2 * (-1.0 / 720 + m2 * (1.0 / 40320))))
    odd = (quad & 1) == 1
    cc = jnp.where(odd, s, c)
    ss = jnp.where(odd, c, s)
    cos = jnp.where((quad == 1) | (quad == 2), -cc, cc)
    sin = jnp.where((quad == 2) | (quad == 3), -ss, ss)
    return cos, sin


def iota(shape, dim):
    return lax.broadcasted_iota(jnp.int32, shape, dim)


def prep_kernel(chirp_ref, taps_ref, slots_ref, mc_ref, a_ref, d0_ref, i12_ref, d12_ref):
    leaf = lax.axis_index("leaf")
    turn = lax.axis_index("turn")
    core = leaf % 2
    sq = (BEAMS, BEAMS)

    g = jnp.broadcast_to(chirp_ref[...][:, None, :], (2, 8, 128)).reshape(16, 128)
    flip = ((iota(sq, 0) + iota(sq, 1)) % 128 == 0).astype(bf16)
    h = jnp.dot(g, flip, preferred_element_type=f32)
    lower = iota(sq, 0) >= iota(sq, 1)
    tabs = []
    for part in range(2):
        row = jnp.broadcast_to(h[8 * part : 8 * part + 1], sq)
        tabs.append(pltpu.roll(row, 0, 1, stride=1, stride_axis=0))
    for side in range(2):
        re, im = (jnp.where(lower if side == 0 else ~lower, t, 0.0) for t in tabs)
        at = 256 * side
        mc_ref[0:128, at : at + 128] = re.astype(bf16)
        mc_ref[0:128, at + 128 : at + 256] = im.astype(bf16)
        mc_ref[128:256, at : at + 128] = (-im).astype(bf16)
        mc_ref[128:256, at + 128 : at + 256] = re.astype(bf16)

    def interp(level, side):
        rows = taps_ref[level, side]
        cells = iota(sq, 1)
        total = jnp.zeros(sq, f32)
        for t in range(TAPS):
            total = total + jnp.where(rows[:, t : t + 1] == cells, WEIGHTS[t], 0.0)
        return total.astype(bf16)

    slot = slots_ref[0, turn]
    beam = iota(sq, 0)
    lane = iota(sq, 1)
    m = lane % SUBP
    n = (2 * beam + 1 - BEAMS) * (2 * m + 1 - SUBP) + 3 * (beam + 1) * (2 * slot + 1) * (2 * m + 1)
    cos, sin = cos_sin(8 * n)
    scale = 1.0 / math.sqrt(2.0 * NSUB * SUBP)
    cos, sin = cos * scale, sin * scale
    first = lane < SUBP
    s_re = jnp.where(first, cos, -sin).astype(bf16)
    s_im = jnp.where(first, sin, cos).astype(bf16)
    i0 = interp(0, core)
    z_re = jnp.dot(i0, s_re, preferred_element_type=f32)
    z_im = jnp.dot(i0, s_im, preferred_element_type=f32)
    ca, sa = cos_sin(beam * beam * (core + 1))
    a_ref[0:128] = (ca * z_re - sa * z_im).astype(bf16)
    a_ref[128:256] = (ca * z_im + sa * z_re).astype(bf16)

    big = (BEAMS, COLS)
    bins = iota(big, 1) + COLS * core + 1
    odd = 2 * iota(big, 0) + 1 - BEAMS
    sign = (2 * core - 1).astype(f32)
    for par in range(2):
        c, s = cos_sin(2 * odd * (bins + 1024 * par))
        d0_ref[0, par] = c
        d0_ref[1, par] = s * sign

    bins = bins + 1024 * turn
    for level in (1, 2):
        side = (leaf >> level) % 2
        i12_ref[level - 1] = interp(level, side)
        square = iota(big, 0) * iota(big, 0)
        c, s = cos_sin(odd * bins * ((2 * side - 1) * (level + 2)) + square * (side + 1))
        d12_ref[level - 1, 0] = c
        d12_ref[level - 1, 1] = s


def prepare(chirp, taps, slots):
    vmem = pl.BlockSpec(memory_space=pltpu.VMEM)
    return pl.pallas_call(
        prep_kernel,
        out_shape=(
            jax.ShapeDtypeStruct((256, 512), bf16),
            jax.ShapeDtypeStruct((256, 128), bf16),
            jax.ShapeDtypeStruct((2, 2, BEAMS, COLS), f32),
            jax.ShapeDtypeStruct((2, BEAMS, BEAMS), bf16),
            jax.ShapeDtypeStruct((2, 2, BEAMS, COLS), f32),
        ),
        in_specs=[vmem, vmem, pl.BlockSpec(memory_space=pltpu.SMEM)],
        out_specs=(vmem,) * 5,
        name="prepare",
    )(chirp, taps, slots)


def main_kernel(
    x_ref, mc_ref, a_ref, d0_ref, i12_ref, d12_ref, out_ref,
    xbuf, u, edge, xb, aoth, ay, az,
    rby, sby, rbz, sbz, rb2, sb2, rb3, sb3, img, vout, rl,
    in_sem, ex_s, ex_r, a_s, a_r, y_s, y_r, z_s, z_r, s2_s, s2_r, s3_s, s3_r, l_s, l_r,
):
    leaf = lax.axis_index("leaf")
    turn = lax.axis_index("turn")
    core = leaf % 2
    z = turn // NY
    y = turn % NY
    mate = leaf + 1 - 2 * core

    def turn_at(zz, yy):
        return (zz % NZ) * NY + yy % NY

    ynbr = (turn_at(z, y + 1), turn_at(z, y + NY - 1))
    znbr = (turn_at(z + 1, y), turn_at(z + NZ - 1, y))

    def pull(gi, slot):
        at = pl.multiple_of(gi * GRAN, GRAN)
        return pltpu.make_async_copy(x_ref.at[:, pl.ds(at, GRAN), :], xbuf.at[slot], in_sem.at[slot])

    pull(NGRAN - 1, 0).start()

    barrier = pltpu.get_barrier_semaphore()
    for t in ynbr + znbr:
        pl.semaphore_signal(barrier, inc=1, device_id={"turn": t}, device_id_type=MESH)
    for e in range(1, NLEAF):
        pl.semaphore_signal(barrier, inc=1, device_id={"leaf": (leaf + e) % NLEAF}, device_id_type=MESH)
    pl.semaphore_wait(barrier, 4 + NLEAF - 1)

    def remote(src, dst, ssem, rsem, where):
        return pltpu.make_async_remote_copy(
            src_ref=src, dst_ref=dst, send_sem=ssem, recv_sem=rsem,
            device_id=where, device_id_type=MESH,
        )

    a_copy = remote(a_ref, aoth, a_s, a_r, {"leaf": mate})
    a_copy.start()

    def exchange(gi):
        pair = pl.ds(2 * gi, 2)
        return remote(xb.at[pair, 2], xb.at[pair, 1], ex_s.at[gi], ex_r.at[gi], {"leaf": mate})

    edge[...] = jnp.zeros_like(edge)

    def granule(step, carry):
        gi = NGRAN - 1 - step
        slot = step % 2

        @pl.when(step + 1 < NGRAN)
        def _():
            pull(gi - 1, 1 - slot).start()

        pull(gi, slot).wait()
        for hf in range(2):
            rows = xbuf[slot, pl.ds(32 * hf, 32)].reshape(32 * GRAN, 256)
            prod = jnp.dot(rows, mc_ref[...], preferred_element_type=f32)
            for q in range(4):
                u[q, 512 * hf : 512 * hf + 512, :] = prod[:, 128 * q : 128 * q + 128]
        for b in range(GRAN):
            half = b % 8 // 4
            plane = 2 * (core if half == 0 else 1 - core)
            tile = 2 * gi + b // 8
            at = 128 * (b % 4)
            for q in range(2):
                own = u[q, pl.ds(b, SUBP, stride=GRAN), :]
                if b == GRAN - 1:
                    nxt = edge[q]
                else:
                    nxt = u[2 + q, pl.ds(b + 1, SUBP, stride=GRAN), :]
                xb[tile, plane, 64 * q : 64 * q + 64, at : at + 128] = (own + nxt).astype(bf16)
        for q in range(2):
            edge[q] = u[2 + q, pl.ds(0, SUBP, stride=GRAN), :]
        exchange(gi).start()
        return carry

    lax.fori_loop(0, NGRAN, granule, 0)

    a_copy.wait()
    for ref, low, count in ((ay, 0, BY), (az, BY, BZ)):
        for part in range(2):
            rows = slice(128 * part + low, 128 * part + low + count)
            mine, other = a_ref[rows], aoth[rows]
            ref[part * count : (part + 1) * count, 0:128] = mine
            ref[part * count : (part + 1) * count, 128:256] = other
            ref[(2 + part) * count : (3 + part) * count, 0:128] = mine
            ref[(2 + part) * count : (3 + part) * count, 128:256] = -other

    rby[:, 12] = jnp.zeros((2, BY, WIDE), bf16)
    rbz[:, 14] = jnp.zeros((2, BZ, WIDE), bf16)
    for d in range(2):
        unsent = slice(COLS, WIDE) if d == 0 else slice(0, COLS)
        rb2[d, 0, :, unsent] = jnp.zeros((BY, COLS), bf16)
        rb3[d, 0, :, unsent] = jnp.zeros((BZ, COLS), bf16)

    def drain(gi, carry):
        exchange(gi).wait()
        return carry

    lax.fori_loop(0, NGRAN, drain, 0)

    def partial_image(ref, low, count, tile, adds, put):
        par = tile % 2
        beams = slice(low, low + count)
        for at in range(0, COLS, 256):
            cols = slice(at, at + 256)
            imag = slice(COLS + at, COLS + at + 256)
            data = xb[tile, 0:2, :, cols].reshape(256, 256)
            r = jnp.dot(ref[...], data, preferred_element_type=f32)
            c, s = d0_ref[0, par, beams, cols], d0_ref[1, par, beams, cols]
            re = c * r[0:count] - s * r[3 * count :]
            im = c * r[count : 2 * count] + s * r[2 * count : 3 * count]
            for got in adds:
                re = re + got[:, cols].astype(f32)
                im = im + got[:, imag].astype(f32)
            put(cols, re)
            put(imag, im)

    def put_to(ref):
        def put(cols, value):
            ref[:, cols] = value.astype(ref.dtype)
        return put

    def order(i, n):
        step = (i + 1) // 2
        return n // 2 + (1 - 2 * (i % 2)) * step

    def y_copy(d, k):
        return remote(sby.at[d, k], rby.at[d, k], y_s.at[d, k], y_r.at[d, k], {"turn": ynbr[d]})

    def z_copy(d, k):
        return remote(sbz.at[d, k], rbz.at[d, k], z_s.at[d, k], z_r.at[d, k], {"turn": znbr[d]})

    def y_message(d, k):
        far = k < 4
        away = jnp.where(far, 2, 1)
        i = jnp.where(far, k + 4 * d, k - 4)
        yy = y + away if d == 0 else y + NY - away
        tile = turn_at(z + order(i, NZ), yy)
        base = 4 + 4 * d
        takes = (k >= base) & (k < base + 4)
        src = jnp.where(takes, k - base, 12)

        @pl.when(takes)
        def _():
            y_copy(d, k - base).wait_recv()

        partial_image(ay, 0, BY, tile, (rby.at[d, src],), put_to(sby.at[d, k]))
        y_copy(d, k).start()

    def z_message(d, k):
        away = 4 - (k + 2) // 4
        i = (k + 2) % 4
        if d == 0:
            i = jnp.where(k < 2, k, i)
        zz = z + away if d == 0 else z + NZ - away
        tile = turn_at(zz, y + order(i, NY))
        if d == 0:
            takes = ((k >= 2) & (k < 4)) | (k >= 6)
            prev = jnp.where(k < 4, k - 2, k - 4)
        else:
            takes = k >= 4
            prev = k - 4
        src = jnp.where(takes, prev, 14)

        @pl.when(takes)
        def _():
            z_copy(d, prev).wait_recv()

        partial_image(az, BY, BZ, tile, (rbz.at[d, src],), put_to(sbz.at[d, k]))
        z_copy(d, k).start()

    def slot_loop(k, carry):
        @pl.when(k < 12)
        def _():
            for d in range(2):
                y_message(d, k)

        for d in range(2):
            z_message(d, k)
        return carry

    lax.fori_loop(0, 14, slot_loop, 0)

    halves = (slice(0, COLS), slice(COLS, WIDE))

    def far2(d):
        part = halves[d]
        return remote(sb2.at[d, 0, :, part], rb2.at[d, 0, :, part], s2_s.at[d, 0], s2_r.at[d, 0], {"turn": znbr[d]})

    def near2(d, k):
        return remote(sb2.at[d, k], rb2.at[d, k], s2_s.at[d, k], s2_r.at[d, k], {"turn": znbr[d]})

    def far3(d):
        part = halves[d]
        return remote(sb3.at[d, 0, :, part], rb3.at[d, 0, :, part], s3_s.at[d, 0], s3_r.at[d, 0], {"turn": ynbr[d]})

    def near3(d, k):
        return remote(sb3.at[d, k], rb3.at[d, k], s3_s.at[d, k], s3_r.at[d, k], {"turn": ynbr[d]})

    def wait_y(i):
        for d in range(2):
            y_copy(d, 4 + i).wait_recv()
        return (rby.at[0, 4 + i], rby.at[1, 4 + i])

    def wait_z(i):
        for d in range(2):
            z_copy(d, 10 + i).wait_recv()
        return (rbz.at[0, 10 + i], rbz.at[1, 10 + i])

    def put_both(ref):
        def put(cols, value):
            d = 0 if cols.start < COLS else 1
            ref[d, 0, :, cols] = value.astype(bf16)
        return put

    partial_image(ay, 0, BY, turn_at(z + 4, y), wait_y(0), put_both(sb2))
    for d in range(2):
        far2(d).start()

    def second_y(d, q):
        i = 2 * q + 1 + d
        adds = wait_y(i)

        @pl.when(q == 0)
        def _():
            far2(d).wait_recv()

        @pl.when(q > 0)
        def _():
            near2(d, q).wait_recv()

        partial_image(ay, 0, BY, turn_at(z + order(i, NZ), y), adds + (rb2.at[d, q],), put_to(sb2.at[d, q + 1]))
        near2(d, q + 1).start()

    def second_z(i):
        adds = wait_z(i)
        tile = turn_at(z, y + (2, 1, 3, 0)[i])
        if i == 0:
            partial_image(az, BY, BZ, tile, adds, put_both(sb3))
            for d in range(2):
                far3(d).start()
        elif i < 3:
            d = i - 1
            far3(d).wait_recv()
            partial_image(az, BY, BZ, tile, adds + (rb3.at[d, 0],), put_to(sb3.at[d, 1]))
            near3(d, 1).start()
        else:
            for d in range(2):
                near3(d, 1).wait_recv()
            adds = adds + (rb3.at[0, 1], rb3.at[1, 1])
            partial_image(az, BY, BZ, tile, adds, put_to(img.at[pl.ds(BY, BZ)]))

    def second_loop(q, carry):
        for d in range(2):
            second_y(d, q)
        return carry

    lax.fori_loop(0, 2, second_loop, 0)
    for i in range(3):
        second_z(i)
    lax.fori_loop(2, 3, second_loop, 0)
    second_z(3)
    adds = wait_y(7)
    for d in range(2):
        near2(d, 3).wait_recv()
    partial_image(ay, 0, BY, turn, adds + (rb2.at[0, 3], rb2.at[1, 3]), put_to(img.at[pl.ds(0, BY)]))

    for level in range(2):
        value = img[...]
        high = value.astype(bf16)
        low = (value - high.astype(f32)).astype(bf16)
        matrix = i12_ref[level]
        moved = jnp.dot(matrix, high, preferred_element_type=f32) + jnp.dot(matrix, low, preferred_element_type=f32)
        c, s = d12_ref[level, 0], d12_ref[level, 1]
        re = c * moved[:, :COLS] - s * moved[:, COLS:]
        im = c * moved[:, COLS:] + s * moved[:, :COLS]
        target = img if level == 0 else vout
        target[:, :COLS] = re.astype(target.dtype)
        target[:, COLS:] = im.astype(target.dtype)

    def share(e):
        to = (leaf + e) % NLEAF
        rows = pl.ds(pl.multiple_of(16 * to, 16), 16)
        return remote(vout.at[rows], rl.at[leaf], l_s.at[e - 1], l_r.at[e - 1], {"leaf": to})

    def shared(e):
        src = (leaf + NLEAF - e) % NLEAF
        return remote(vout.at[pl.ds(0, 16)], rl.at[src], l_s.at[e - 1], l_r.at[e - 1], {"leaf": mate})

    for e in range(1, NLEAF):
        share(e).start()
    rl[leaf] = vout[pl.ds(pl.multiple_of(16 * leaf, 16), 16)]
    for e in range(1, NLEAF):
        shared(e).wait_recv()
    for side in range(2):
        total = rl[side].astype(f32)
        for xx in range(1, 4):
            total = total + rl[2 * xx + side].astype(f32)
        total = total.astype(bf16)
        for b in range(4):
            out_ref[4 * side + b, :, 0:128] = total[:, 128 * b : 128 * b + 128]
            out_ref[4 * side + b, :, 128:256] = total[:, COLS + 128 * b : COLS + 128 * b + 128]

    def sent_y(k, carry):
        for d in range(2):
            y_copy(d, k).wait_send()
        return carry

    def sent_z(k, carry):
        for d in range(2):
            z_copy(d, k).wait_send()
        return carry

    lax.fori_loop(0, 12, sent_y, 0)
    lax.fori_loop(0, 14, sent_z, 0)
    for d in range(2):
        far2(d).wait_send()
        far3(d).wait_send()
        near3(d, 1).wait_send()
        for k in range(1, 4):
            near2(d, k).wait_send()
    for e in range(1, NLEAF):
        share(e).wait_send()


def reduce_merge(x, mc, a, d0, i12, d12):
    vmem = pl.BlockSpec(memory_space=pltpu.VMEM)
    dma = pltpu.SemaphoreType.DMA
    return pl.pallas_call(
        main_kernel,
        out_shape=jax.ShapeDtypeStruct((8, 16, 256), bf16),
        in_specs=[pl.BlockSpec(memory_space=pl.ANY)] + [vmem] * 5,
        out_specs=vmem,
        scratch_shapes=[
            pltpu.VMEM((2, SUBP, GRAN, 256), bf16),
            pltpu.VMEM((4, SUBP * GRAN, 128), f32),
            pltpu.VMEM((2, SUBP, 128), f32),
            pltpu.VMEM((TILES, 3, 128, COLS), bf16),
            pltpu.VMEM((256, 128), bf16),
            pltpu.VMEM((4 * BY, 256), bf16),
            pltpu.VMEM((4 * BZ, 256), bf16),
            pltpu.VMEM((2, 13, BY, WIDE), bf16),
            pltpu.VMEM((2, 12, BY, WIDE), bf16),
            pltpu.VMEM((2, 15, BZ, WIDE), bf16),
            pltpu.VMEM((2, 14, BZ, WIDE), bf16),
            pltpu.VMEM((2, 4, BY, WIDE), bf16),
            pltpu.VMEM((2, 4, BY, WIDE), bf16),
            pltpu.VMEM((2, 2, BZ, WIDE), bf16),
            pltpu.VMEM((2, 2, BZ, WIDE), bf16),
            pltpu.VMEM((BEAMS, WIDE), f32),
            pltpu.VMEM((BEAMS, WIDE), bf16),
            pltpu.VMEM((NLEAF, 16, WIDE), bf16),
            dma((2,)), dma((NGRAN,)), dma((NGRAN,)), dma, dma,
            dma((2, 12)), dma((2, 12)), dma((2, 14)), dma((2, 14)),
            dma((2, 4)), dma((2, 4)), dma((2, 2)), dma((2, 2)),
            dma((NLEAF - 1,)), dma((NLEAF - 1,)),
        ],
        compiler_params=pltpu.CompilerParams(
            collective_id=0, has_side_effects=True, vmem_limit_bytes=60 * 1024 * 1024
        ),
        name="reduce_merge",
    )(x, mc, a, d0, i12, d12)


def per_device(echoes, chirp, taps, slots):
    tables = prepare(chirp, taps, slots)
    image = reduce_merge(echoes, *tables)
    return jnp.transpose(image, (1, 0, 2))


def solution(mesh):
    placed = (P(("leaf", "turn"), None, None), P(), P(), P("leaf", None))
    return jax.shard_map(
        per_device, mesh=mesh, in_specs=placed, out_specs=P("leaf", "turn", None), check_vma=False
    )
```

profile of v0, /device:TPU:1, one launch (start us, length us, event | category | flops | bytes accessed | tf_op | source)
XLA Modules:
  0.0 96.7 jit_solution(5188238548041663290)
XLA Ops:
  0.0 1.7 %copy.5.taps_ref = s32[3,2,128,8]{3,2,1,0:T(8,128)} copy(s32[3,2,128,8]{2,3,1,0:T(8,128)} %param.6) | data formatting | bytes 49152 | tf_op args[2]
  1.7 4.3 %prepare.1 = (bf16[256,512]{1,0:T(8,128)(2,1)}, bf16[256,128]{1,0:T(8,128)(2,1)}, f32[2,2,128,512]{3,2,1,0:T(8,128)}, bf16[2,128,128]{2,1,0:T(8,128)(2,1)}, f32[2,2,128,512]{3,2,1,0:T(8,128)}) custom-call(bf16[2,128]{1,0:T(2,128)(2,1)} %chirp_ref.1, s32[3,2,128,8]{3,2,1,0:T(8,128)} %copy.5.taps_ref, s32[1,32]{1,0:T(1,128)} %slots_ref.1), custom_call_target="tpu_custom_call" | custom-call | tf_op jit(solution)/shard_map/prepare/pallas_call | solution.py:121
  6.0 89.2 %reduce_merge.1 = bf16[8,16,256]{2,1,0:T(8,128)(2,1)} custom-call(bf16[64,256,256]{2,1,0:T(8,128)(2,1)} %x_ref.1, bf16[256,512]{1,0:T(8,128)(2,1)} %get-tuple-element.10.mc_ref, bf16[256,128]{1,0:T(8,128)(2,1)} %get-tuple-element.11.a_ref, f32[2,2,128,512]{3,2,1,0:T(8,128)} %get-tuple-element.12.d0_ref, bf16[2,128,128]{2,1,0:T(8,128)(2,1)} %get-tuple-element.13.i12_ref, ...), custom_call_target="tpu_custom_call" | custom-call | tf_op jit(solution)/shard_map/reduce_merge/pallas_call | solution.py:467
  95.2 1.5 %copy.6 = bf16[16,8,256]{2,1,0:T(8,128)(2,1)} copy(bf16[16,8,256]{2,0,1:T(8,128)(2,1)} %bitcast.1) | data formatting | bytes 131072 | tf_op jit(solution)/shard_map/transpose | solution.py:506
where the time goes:
time: 97.2 us; the launch traced here: 96.7 us
  Pallas kernels  93.5 us (96%)
  local copies, waits for them, and re-layouts  3.15 us (3%)
    pallas_call x1, Pallas kernels, reduce_merge(): pl.pallas_call(main_kernel, out_shape=jax.ShapeDtypeStruct((8, 16, 256),...  89.2 us
    pallas_call x1, Pallas kernels, prepare(): pl.pallas_call(prep_kernel, out_shape=(jax.ShapeDtypeStruct((256, 512), b...  4.34 us

commit v1 on v0

--- a/solution.py
+++ b/solution.py
@@ -135,9 +135,9 @@
 
 def main_kernel(
     x_ref, mc_ref, a_ref, d0_ref, i12_ref, d12_ref, out_ref,
-    xbuf, u, edge, xb, aoth, ay, az,
+    xbuf, ebuf, u, edge, edges, xb, aoth, ay, az,
     rby, sby, rbz, sbz, rb2, sb2, rb3, sb3, img, vout, rl,
-    in_sem, ex_s, ex_r, a_s, a_r, y_s, y_r, z_s, z_r, s2_s, s2_r, s3_s, s3_r, l_s, l_r,
+    in_sem, e_sem, ex_s, ex_r, a_s, a_r, y_s, y_r, z_s, z_r, s2_s, s2_r, s3_s, s3_r, l_s, l_r,
 ):
     leaf = lax.axis_index("leaf")
     turn = lax.axis_index("turn")
@@ -152,11 +152,25 @@
     ynbr = (turn_at(z, y + 1), turn_at(z, y + NY - 1))
     znbr = (turn_at(z + 1, y), turn_at(z + NZ - 1, y))
 
-    def pull(gi, slot):
-        at = pl.multiple_of(gi * GRAN, GRAN)
-        return pltpu.make_async_copy(x_ref.at[:, pl.ds(at, GRAN), :], xbuf.at[slot], in_sem.at[slot])
-
-    pull(NGRAN - 1, 0).start()
+    def order(i, n):
+        step = (i + 1) // 2
+        return n // 2 + (1 - 2 * (i % 2)) * step
+
+    def chunk(i):
+        return (z + order(i, NZ)) % NZ
+
+    def pull(i, g):
+        at = pl.multiple_of((2 * chunk(i) + 1 - g) * GRAN, GRAN)
+        return pltpu.make_async_copy(x_ref.at[:, pl.ds(at, GRAN), :], xbuf.at[i % 2, g], in_sem.at[i % 2, g])
+
+    def pull_edge(i):
+        at = pl.multiple_of((chunk(i) + 1) % NZ * 2 * GRAN, 8)
+        slot = i // 2 % 2
+        return pltpu.make_async_copy(x_ref.at[:, pl.ds(at, 8), :], ebuf.at[slot], e_sem.at[slot])
+
+    pull_edge(0).start()
+    for g in range(2):
+        pull(0, g).start()
 
     barrier = pltpu.get_barrier_semaphore()
     for t in ynbr + znbr:
@@ -174,44 +188,69 @@
     a_copy = remote(a_ref, aoth, a_s, a_r, {"leaf": mate})
     a_copy.start()
 
-    def exchange(gi):
-        pair = pl.ds(2 * gi, 2)
-        return remote(xb.at[pair, 2], xb.at[pair, 1], ex_s.at[gi], ex_r.at[gi], {"leaf": mate})
-
-    edge[...] = jnp.zeros_like(edge)
-
-    def granule(step, carry):
-        gi = NGRAN - 1 - step
-        slot = step % 2
-
-        @pl.when(step + 1 < NGRAN)
-        def _():
-            pull(gi - 1, 1 - slot).start()
-
-        pull(gi, slot).wait()
+    def exchange(i):
+        four = pl.ds(4 * chunk(i), 4)
+        return remote(xb.at[four, 2], xb.at[four, 1], ex_s.at[i], ex_r.at[i], {"leaf": mate})
+
+    def granule(i, g):
+        pull(i, g).wait()
+        gi = 2 * chunk(i) + 1 - g
         for hf in range(2):
-            rows = xbuf[slot, pl.ds(32 * hf, 32)].reshape(32 * GRAN, 256)
-            prod = jnp.dot(rows, mc_ref[...], preferred_element_type=f32)
+            rows = xbuf[i % 2, g, pl.ds(32 * hf, 32)].reshape(32 * GRAN, 256)
+            prod = jnp.dot(rows, mc_ref[...], preferred_element_type=f32).reshape(32, 2, 8, 512)
             for q in range(4):
-                u[q, 512 * hf : 512 * hf + 512, :] = prod[:, 128 * q : 128 * q + 128]
+                for e in range(2):
+                    part = prod[:, e, :, 128 * q : 128 * q + 128].reshape(256, 128)
+                    u[q, e, 256 * hf : 256 * hf + 256, :] = part
         for b in range(GRAN):
             half = b % 8 // 4
             plane = 2 * (core if half == 0 else 1 - core)
             tile = 2 * gi + b // 8
             at = 128 * (b % 4)
             for q in range(2):
-                own = u[q, pl.ds(b, SUBP, stride=GRAN), :]
+                own = u[q, b // 8, pl.ds(b % 8, SUBP, stride=8), :]
                 if b == GRAN - 1:
                     nxt = edge[q]
                 else:
-                    nxt = u[2 + q, pl.ds(b + 1, SUBP, stride=GRAN), :]
+                    nxt = u[2 + q, (b + 1) // 8, pl.ds((b + 1) % 8, SUBP, stride=8), :]
                 xb[tile, plane, 64 * q : 64 * q + 64, at : at + 128] = (own + nxt).astype(bf16)
         for q in range(2):
-            edge[q] = u[2 + q, pl.ds(0, SUBP, stride=GRAN), :]
-        exchange(gi).start()
-        return carry
-
-    lax.fori_loop(0, NGRAN, granule, 0)
+            edge[q] = u[2 + q, 0, pl.ds(0, SUBP, stride=8), :]
+
+    def compress(i):
+        @pl.when(i + 1 < NZ)
+        def _():
+            for g in range(2):
+                pull(i + 1, g).start()
+
+        @pl.when((i % 2 == 1) & (i + 1 < NZ))
+        def _():
+            pull_edge(i + 1).start()
+
+        here = chunk(i)
+
+        @pl.when(i % 2 == 0)
+        def _():
+            pull_edge(i).wait()
+            rows = ebuf[i // 2 % 2].reshape(SUBP * 8, 256)
+            prod = jnp.dot(rows, mc_ref[:, 256:512], preferred_element_type=f32)
+            for q in range(2):
+                u[q, 0] = prod[:, 128 * q : 128 * q + 128]
+            for q in range(2):
+                edges[(here + 1) % NZ, q] = u[q, 0, pl.ds(0, SUBP, stride=8), :]
+
+        edge[...] = edges[here + 1]
+
+        def both(g, carry):
+            granule(i, g)
+            return carry
+
+        lax.fori_loop(0, 2, both, 0)
+        edges[here] = edge[...]
+        exchange(i).start()
+
+    edges[NZ] = jnp.zeros((2, SUBP, 128), f32)
+    compress(0)
 
     a_copy.wait()
     for ref, low, count in ((ay, 0, BY), (az, BY, BZ)):
@@ -229,12 +268,6 @@
         unsent = slice(COLS, WIDE) if d == 0 else slice(0, COLS)
         rb2[d, 0, :, unsent] = jnp.zeros((BY, COLS), bf16)
         rb3[d, 0, :, unsent] = jnp.zeros((BZ, COLS), bf16)
-
-    def drain(gi, carry):
-        exchange(gi).wait()
-        return carry
-
-    lax.fori_loop(0, NGRAN, drain, 0)
 
     def partial_image(ref, low, count, tile, adds, put):
         par = tile % 2
@@ -258,82 +291,67 @@
             ref[:, cols] = value.astype(ref.dtype)
         return put
 
-    def order(i, n):
-        step = (i + 1) // 2
-        return n // 2 + (1 - 2 * (i % 2)) * step
+    def y_to(d):
+        return turn_at(z, y + 1 + 2 * d)
+
+    def z_to(d):
+        return turn_at(z + 1 + (NZ - 2) * d, y)
 
     def y_copy(d, k):
-        return remote(sby.at[d, k], rby.at[d, k], y_s.at[d, k], y_r.at[d, k], {"turn": ynbr[d]})
+        return remote(sby.at[d, k], rby.at[d, k], y_s.at[d, k], y_r.at[d, k], {"turn": y_to(d)})
 
     def z_copy(d, k):
-        return remote(sbz.at[d, k], rbz.at[d, k], z_s.at[d, k], z_r.at[d, k], {"turn": znbr[d]})
-
-    def y_message(d, k):
-        far = k < 4
-        away = jnp.where(far, 2, 1)
-        i = jnp.where(far, k + 4 * d, k - 4)
-        yy = y + away if d == 0 else y + NY - away
-        tile = turn_at(z + order(i, NZ), yy)
-        base = 4 + 4 * d
-        takes = (k >= base) & (k < base + 4)
-        src = jnp.where(takes, k - base, 12)
+        return remote(sbz.at[d, k], rbz.at[d, k], z_s.at[d, k], z_r.at[d, k], {"turn": z_to(d)})
+
+    def y_message(c, near, d):
+        k = jnp.where(near == 1, 4 + c, c // 2)
+        takes = (near == 1) & (c % 2 == d)
+        src = jnp.where(takes, c // 2, 12)
 
         @pl.when(takes)
         def _():
-            y_copy(d, k - base).wait_recv()
-
+            y_copy(d, c // 2).wait_recv()
+
+        tile = turn_at(chunk(c), y + 2 + near * (2 * d - 1))
         partial_image(ay, 0, BY, tile, (rby.at[d, src],), put_to(sby.at[d, k]))
         y_copy(d, k).start()
 
-    def z_message(d, k):
-        away = 4 - (k + 2) // 4
-        i = (k + 2) % 4
-        if d == 0:
-            i = jnp.where(k < 2, k, i)
-        zz = z + away if d == 0 else z + NZ - away
-        tile = turn_at(zz, y + order(i, NY))
-        if d == 0:
-            takes = ((k >= 2) & (k < 4)) | (k >= 6)
-            prev = jnp.where(k < 4, k - 2, k - 4)
-        else:
-            takes = k >= 4
-            prev = k - 4
+    def z_far(d, j):
+        tile = turn_at(chunk(0), y + order(j + 2 * d, NY))
+        partial_image(az, BY, BZ, tile, (), put_to(sbz.at[d, j]))
+        z_copy(d, j).start()
+
+    def z_near(c, j):
+        d = (c + 1) % 2
+        step = (c - 1) // 2
+        k = 2 + 4 * step + j
+        takes = (step > 0) | (j // 2 == d)
+        prev = jnp.where(step > 0, k - 4, j - 2 * d)
         src = jnp.where(takes, prev, 14)
 
         @pl.when(takes)
         def _():
             z_copy(d, prev).wait_recv()
 
+        tile = turn_at(chunk(c), y + order(j, NY))
         partial_image(az, BY, BZ, tile, (rbz.at[d, src],), put_to(sbz.at[d, k]))
         z_copy(d, k).start()
 
-    def slot_loop(k, carry):
-        @pl.when(k < 12)
-        def _():
-            for d in range(2):
-                y_message(d, k)
-
-        for d in range(2):
-            z_message(d, k)
-        return carry
-
-    lax.fori_loop(0, 14, slot_loop, 0)
-
     halves = (slice(0, COLS), slice(COLS, WIDE))
 
     def far2(d):
         part = halves[d]
-        return remote(sb2.at[d, 0, :, part], rb2.at[d, 0, :, part], s2_s.at[d, 0], s2_r.at[d, 0], {"turn": znbr[d]})
+        return remote(sb2.at[d, 0, :, part], rb2.at[d, 0, :, part], s2_s.at[d, 0], s2_r.at[d, 0], {"turn": z_to(d)})
 
     def near2(d, k):
-        return remote(sb2.at[d, k], rb2.at[d, k], s2_s.at[d, k], s2_r.at[d, k], {"turn": znbr[d]})
+        return remote(sb2.at[d, k], rb2.at[d, k], s2_s.at[d, k], s2_r.at[d, k], {"turn": z_to(d)})
 
     def far3(d):
         part = halves[d]
-        return remote(sb3.at[d, 0, :, part], rb3.at[d, 0, :, part], s3_s.at[d, 0], s3_r.at[d, 0], {"turn": ynbr[d]})
+        return remote(sb3.at[d, 0, :, part], rb3.at[d, 0, :, part], s3_s.at[d, 0], s3_r.at[d, 0], {"turn": y_to(d)})
 
     def near3(d, k):
-        return remote(sb3.at[d, k], rb3.at[d, k], s3_s.at[d, k], s3_r.at[d, k], {"turn": ynbr[d]})
+        return remote(sb3.at[d, k], rb3.at[d, k], s3_s.at[d, k], s3_r.at[d, k], {"turn": y_to(d)})
 
     def wait_y(i):
         for d in range(2):
@@ -351,23 +369,25 @@
             ref[d, 0, :, cols] = value.astype(bf16)
         return put
 
-    partial_image(ay, 0, BY, turn_at(z + 4, y), wait_y(0), put_both(sb2))
-    for d in range(2):
-        far2(d).start()
-
-    def second_y(d, q):
-        i = 2 * q + 1 + d
+    def second_far():
+        partial_image(ay, 0, BY, turn_at(z + 4, y), wait_y(0), put_both(sb2))
+        for d in range(2):
+            far2(d).start()
+
+    def second_y(i):
+        d = (i + 1) % 2
+        q = (i - 1) // 2
         adds = wait_y(i)
-
-        @pl.when(q == 0)
-        def _():
-            far2(d).wait_recv()
+        for side in range(2):
+            @pl.when((q == 0) & (d == side))
+            def _():
+                far2(side).wait_recv()
 
         @pl.when(q > 0)
         def _():
             near2(d, q).wait_recv()
 
-        partial_image(ay, 0, BY, turn_at(z + order(i, NZ), y), adds + (rb2.at[d, q],), put_to(sb2.at[d, q + 1]))
+        partial_image(ay, 0, BY, turn_at(chunk(i), y), adds + (rb2.at[d, q],), put_to(sb2.at[d, q + 1]))
         near2(d, q + 1).start()
 
     def second_z(i):
@@ -388,15 +408,63 @@
             adds = adds + (rb3.at[0, 1], rb3.at[1, 1])
             partial_image(az, BY, BZ, tile, adds, put_to(img.at[pl.ds(BY, BZ)]))
 
-    def second_loop(q, carry):
-        for d in range(2):
-            second_y(d, q)
+    def main_loop(i, carry):
+        @pl.when(i < NZ)
+        def _():
+            compress(i)
+
+        @pl.when(i <= NZ)
+        def _():
+            c = i - 1
+            exchange(c).wait_recv()
+
+            def pair(near, carry):
+                y_message(c, near, (c + near) % 2)
+                return carry
+
+            lax.fori_loop(0, 2, pair, 0)
+
+        @pl.when(i == 1)
+        def _():
+            def far(n, carry):
+                z_far(n // 2, n % 2)
+                return carry
+
+            lax.fori_loop(0, 4, far, 0)
+
+        @pl.when((i >= 3) & (i <= NZ))
+        def _():
+            def near(j, carry):
+                z_near(i - 2, j)
+                return carry
+
+            lax.fori_loop(0, 4, near, 0)
+
+        @pl.when(i >= 4)
+        def _():
+            y_message(i - 4, 1, i % 2)
+
+        @pl.when(i == NZ)
+        def _():
+            second_far()
+
+        @pl.when(i > NZ)
+        def _():
+            second_y(i - NZ)
+
         return carry
 
-    lax.fori_loop(0, 2, second_loop, 0)
-    for i in range(3):
-        second_z(i)
-    lax.fori_loop(2, 3, second_loop, 0)
+    lax.fori_loop(1, 12, main_loop, 0)
+
+    def second_loop(i, carry):
+        second_y(i)
+        return carry
+
+    second_z(0)
+    lax.fori_loop(4, 5, second_loop, 0)
+    second_z(1)
+    second_z(2)
+    lax.fori_loop(5, 7, second_loop, 0)
     second_z(3)
     adds = wait_y(7)
     for d in range(2):
@@ -449,6 +517,11 @@
             z_copy(d, k).wait_send()
         return carry
 
+    def sent_mate(i, carry):
+        exchange(i).wait_send()
+        return carry
+
+    lax.fori_loop(0, NZ, sent_mate, 0)
     lax.fori_loop(0, 12, sent_y, 0)
     lax.fori_loop(0, 14, sent_z, 0)
     for d in range(2):
@@ -470,9 +543,11 @@
         in_specs=[pl.BlockSpec(memory_space=pl.ANY)] + [vmem] * 5,
         out_specs=vmem,
         scratch_shapes=[
-            pltpu.VMEM((2, SUBP, GRAN, 256), bf16),
-            pltpu.VMEM((4, SUBP * GRAN, 128), f32),
+            pltpu.VMEM((2, 2, SUBP, GRAN, 256), bf16),
+            pltpu.VMEM((2, SUBP, 8, 256), bf16),
+            pltpu.VMEM((4, 2, SUBP * 8, 128), f32),
             pltpu.VMEM((2, SUBP, 128), f32),
+            pltpu.VMEM((NZ + 1, 2, SUBP, 128), f32),
             pltpu.VMEM((TILES, 3, 128, COLS), bf16),
             pltpu.VMEM((256, 128), bf16),
             pltpu.VMEM((4 * BY, 256), bf16),
@@ -488,7 +563,7 @@
             pltpu.VMEM((BEAMS, WIDE), f32),
             pltpu.VMEM((BEAMS, WIDE), bf16),
             pltpu.VMEM((NLEAF, 16, WIDE), bf16),
-            dma((2,)), dma((NGRAN,)), dma((NGRAN,)), dma, dma,
+            dma((2, 2)), dma((2,)), dma((NZ,)), dma((NZ,)), dma, dma,
             dma((2, 12)), dma((2, 12)), dma((2, 14)), dma((2, 14)),
             dma((2, 4)), dma((2, 4)), dma((2, 2)), dma((2, 2)),
             dma((NLEAF - 1,)), dma((NLEAF - 1,)),

time: 97.2 us -> 85.9 us (0.88)
  the two profiles are of different devices: /device:TPU:1 before, /device:TPU:9 now
where the time goes in v1:
time: 85.9 us; the launch traced here: 85.7 us
  Pallas kernels  82.5 us (96%)
  local copies, waits for them, and re-layouts  3.15 us (4%)
    pallas_call x1, Pallas kernels, reduce_merge(): pl.pallas_call(main_kernel, out_shape=jax.ShapeDtypeStruct((8, 16, 256),...  78.2 us
    pallas_call x1, Pallas kernels, prepare(): pl.pallas_call(prep_kernel, out_shape=(jax.ShapeDtypeStruct((256, 512), b...  4.34 us

profile of v1, /device:TPU:9, one launch (start us, length us, event | category | flops | bytes accessed | tf_op | source)
XLA Modules:
  0.0 85.7 jit_solution(9258575341584594785)
XLA Ops:
  0.0 1.7 %copy.5.taps_ref = s32[3,2,128,8]{3,2,1,0:T(8,128)} copy(s32[3,2,128,8]{2,3,1,0:T(8,128)} %param.6) | data formatting | bytes 49152 | tf_op args[2]
  1.7 4.3 %prepare.1 = (bf16[256,512]{1,0:T(8,128)(2,1)}, bf16[256,128]{1,0:T(8,128)(2,1)}, f32[2,2,128,512]{3,2,1,0:T(8,128)}, bf16[2,128,128]{2,1,0:T(8,128)(2,1)}, f32[2,2,128,512]{3,2,1,0:T(8,128)}) custom-call(bf16[2,128]{1,0:T(2,128)(2,1)} %chirp_ref.1, s32[3,2,128,8]{3,2,1,0:T(8,128)} %copy.5.taps_ref, s32[1,32]{1,0:T(1,128)} %slots_ref.1), custom_call_target="tpu_custom_call" | custom-call | tf_op jit(solution)/shard_map/prepare/pallas_call | solution.py:121
  6.0 78.2 %reduce_merge.1 = bf16[8,16,256]{2,1,0:T(8,128)(2,1)} custom-call(bf16[64,256,256]{2,1,0:T(8,128)(2,1)} %x_ref.1, bf16[256,512]{1,0:T(8,128)(2,1)} %get-tuple-element.10.mc_ref, bf16[256,128]{1,0:T(8,128)(2,1)} %get-tuple-element.11.a_ref, f32[2,2,128,512]{3,2,1,0:T(8,128)} %get-tuple-element.12.d0_ref, bf16[2,128,128]{2,1,0:T(8,128)(2,1)} %get-tuple-element.13.i12_ref, ...), custom_call_target="tpu_custom_call" | custom-call | tf_op jit(solution)/shard_map/reduce_merge/pallas_call | solution.py:540
  84.2 1.5 %copy.6 = bf16[16,8,256]{2,1,0:T(8,128)(2,1)} copy(bf16[16,8,256]{2,0,1:T(8,128)(2,1)} %bitcast.1) | data formatting | bytes 131072 | tf_op jit(solution)/shard_map/transpose | solution.py:581

commit v2 on v1

--- a/solution.py
+++ b/solution.py
@@ -49,7 +49,25 @@
     return lax.broadcasted_iota(jnp.int32, shape, dim)
 
 
-def prep_kernel(chirp_ref, taps_ref, slots_ref, mc_ref, a_ref, d0_ref, i12_ref, d12_ref):
+def interp(rows):
+    cells = iota((BEAMS, BEAMS), 0)
+    total = jnp.zeros((BEAMS, BEAMS), f32)
+    for t in range(TAPS):
+        total = total + jnp.where(rows[t : t + 1, :] == cells, WEIGHTS[t], 0.0)
+    return total.T.astype(bf16)
+
+
+def phase_blocks(first, step, count):
+    c, s = cos_sin(first)
+    blocks = [(c, s)]
+    fc, fs = cos_sin(step)
+    for _ in range(count - 1):
+        c, s = c * fc - s * fs, s * fc + c * fs
+        blocks.append((c, s))
+    return blocks
+
+
+def prep_kernel(chirp_ref, taps_ref, slots_ref, mc_ref, a_ref, d0_ref):
     leaf = lax.axis_index("leaf")
     turn = lax.axis_index("turn")
     core = leaf % 2
@@ -71,14 +89,6 @@
         mc_ref[128:256, at : at + 128] = (-im).astype(bf16)
         mc_ref[128:256, at + 128 : at + 256] = re.astype(bf16)
 
-    def interp(level, side):
-        rows = taps_ref[level, side]
-        cells = iota(sq, 1)
-        total = jnp.zeros(sq, f32)
-        for t in range(TAPS):
-            total = total + jnp.where(rows[:, t : t + 1] == cells, WEIGHTS[t], 0.0)
-        return total.astype(bf16)
-
     slot = slots_ref[0, turn]
     beam = iota(sq, 0)
     lane = iota(sq, 1)
@@ -90,30 +100,22 @@
     first = lane < SUBP
     s_re = jnp.where(first, cos, -sin).astype(bf16)
     s_im = jnp.where(first, sin, cos).astype(bf16)
-    i0 = interp(0, core)
+    i0 = interp(taps_ref[0, core])
     z_re = jnp.dot(i0, s_re, preferred_element_type=f32)
     z_im = jnp.dot(i0, s_im, preferred_element_type=f32)
     ca, sa = cos_sin(beam * beam * (core + 1))
     a_ref[0:128] = (ca * z_re - sa * z_im).astype(bf16)
     a_ref[128:256] = (ca * z_im + sa * z_re).astype(bf16)
 
-    big = (BEAMS, COLS)
-    bins = iota(big, 1) + COLS * core + 1
-    odd = 2 * iota(big, 0) + 1 - BEAMS
+    odd = 2 * beam + 1 - BEAMS
     sign = (2 * core - 1).astype(f32)
-    for par in range(2):
-        c, s = cos_sin(2 * odd * (bins + 1024 * par))
-        d0_ref[0, par] = c
-        d0_ref[1, par] = s * sign
-
-    bins = bins + 1024 * turn
-    for level in (1, 2):
-        side = (leaf >> level) % 2
-        i12_ref[level - 1] = interp(level, side)
-        square = iota(big, 0) * iota(big, 0)
-        c, s = cos_sin(odd * bins * ((2 * side - 1) * (level + 2)) + square * (side + 1))
-        d12_ref[level - 1, 0] = c
-        d12_ref[level - 1, 1] = s
+    blocks = phase_blocks(2 * odd * (lane + COLS * core + 1), 2 * odd * 128, COLS // 128)
+    for b, (c, s) in enumerate(blocks):
+        at = slice(128 * b, 128 * b + 128)
+        d0_ref[0, 0, :, at] = c
+        d0_ref[0, 1, :, at] = -c
+        d0_ref[1, 0, :, at] = s * sign
+        d0_ref[1, 1, :, at] = -s * sign
 
 
 def prepare(chirp, taps, slots):
@@ -124,19 +126,17 @@
             jax.ShapeDtypeStruct((256, 512), bf16),
             jax.ShapeDtypeStruct((256, 128), bf16),
             jax.ShapeDtypeStruct((2, 2, BEAMS, COLS), f32),
-            jax.ShapeDtypeStruct((2, BEAMS, BEAMS), bf16),
-            jax.ShapeDtypeStruct((2, 2, BEAMS, COLS), f32),
         ),
         in_specs=[vmem, vmem, pl.BlockSpec(memory_space=pltpu.SMEM)],
-        out_specs=(vmem,) * 5,
+        out_specs=(vmem,) * 3,
         name="prepare",
     )(chirp, taps, slots)
 
 
 def main_kernel(
-    x_ref, mc_ref, a_ref, d0_ref, i12_ref, d12_ref, out_ref,
+    x_ref, mc_ref, a_ref, d0_ref, taps_ref, out_ref,
     xbuf, ebuf, u, edge, edges, xb, aoth, ay, az,
-    rby, sby, rbz, sbz, rb2, sb2, rb3, sb3, img, vout, rl,
+    rby, sby, rbz, sbz, rb2, sb2, rb3, sb3, img, vout, rl, i12, d12,
     in_sem, e_sem, ex_s, ex_r, a_s, a_r, y_s, y_r, z_s, z_r, s2_s, s2_r, s3_s, s3_r, l_s, l_r,
 ):
     leaf = lax.axis_index("leaf")
@@ -422,7 +422,7 @@
                 y_message(c, near, (c + near) % 2)
                 return carry
 
-            lax.fori_loop(0, 2, pair, 0)
+            lax.fori_loop(0, jnp.where(c < 4, 2, 1), pair, 0)
 
         @pl.when(i == 1)
         def _():
@@ -442,7 +442,11 @@
 
         @pl.when(i >= 4)
         def _():
-            y_message(i - 4, 1, i % 2)
+            def pair(n, carry):
+                y_message(i - 4, 1, (i + n) % 2)
+                return carry
+
+            lax.fori_loop(0, jnp.where(i < 8, 1, 2), pair, 0)
 
         @pl.when(i == NZ)
         def _():
@@ -459,6 +463,19 @@
     def second_loop(i, carry):
         second_y(i)
         return carry
+
+    beam = iota((BEAMS, 128), 0)
+    odd = 2 * beam + 1 - BEAMS
+    bins = iota((BEAMS, 128), 1) + 1 + COLS * core + 2 * COLS * turn
+    for level in (1, 2):
+        side = (leaf >> level) % 2
+        i12[level - 1] = interp(taps_ref[level, side])
+        rate = odd * ((2 * side - 1) * (level + 2))
+        blocks = phase_blocks(rate * bins + beam * beam * (side + 1), rate * 128, COLS // 128)
+        for b, (c, s) in enumerate(blocks):
+            at = slice(128 * b, 128 * b + 128)
+            d12[level - 1, 0, :, at] = c
+            d12[level - 1, 1, :, at] = s
 
     second_z(0)
     lax.fori_loop(4, 5, second_loop, 0)
@@ -475,9 +492,9 @@
         value = img[...]
         high = value.astype(bf16)
         low = (value - high.astype(f32)).astype(bf16)
-        matrix = i12_ref[level]
+        matrix = i12[level]
         moved = jnp.dot(matrix, high, preferred_element_type=f32) + jnp.dot(matrix, low, preferred_element_type=f32)
-        c, s = d12_ref[level, 0], d12_ref[level, 1]
+        c, s = d12[level, 0], d12[level, 1]
         re = c * moved[:, :COLS] - s * moved[:, COLS:]
         im = c * moved[:, COLS:] + s * moved[:, :COLS]
         target = img if level == 0 else vout
@@ -534,13 +551,13 @@
         share(e).wait_send()
 
 
-def reduce_merge(x, mc, a, d0, i12, d12):
+def reduce_merge(x, mc, a, d0, taps):
     vmem = pl.BlockSpec(memory_space=pltpu.VMEM)
     dma = pltpu.SemaphoreType.DMA
     return pl.pallas_call(
         main_kernel,
         out_shape=jax.ShapeDtypeStruct((8, 16, 256), bf16),
-        in_specs=[pl.BlockSpec(memory_space=pl.ANY)] + [vmem] * 5,
+        in_specs=[pl.BlockSpec(memory_space=pl.ANY)] + [vmem] * 4,
         out_specs=vmem,
         scratch_shapes=[
             pltpu.VMEM((2, 2, SUBP, GRAN, 256), bf16),
@@ -563,6 +580,8 @@
             pltpu.VMEM((BEAMS, WIDE), f32),
             pltpu.VMEM((BEAMS, WIDE), bf16),
             pltpu.VMEM((NLEAF, 16, WIDE), bf16),
+            pltpu.VMEM((2, BEAMS, BEAMS), bf16),
+            pltpu.VMEM((2, 2, BEAMS, COLS), f32),
             dma((2, 2)), dma((2,)), dma((NZ,)), dma((NZ,)), dma, dma,
             dma((2, 12)), dma((2, 12)), dma((2, 14)), dma((2, 14)),
             dma((2, 4)), dma((2, 4)), dma((2, 2)), dma((2, 2)),
@@ -572,12 +591,13 @@
             collective_id=0, has_side_effects=True, vmem_limit_bytes=60 * 1024 * 1024
         ),
         name="reduce_merge",
-    )(x, mc, a, d0, i12, d12)
+    )(x, mc, a, d0, taps)
 
 
 def per_device(echoes, chirp, taps, slots):
+    taps = jnp.transpose(taps, (0, 1, 3, 2))
     tables = prepare(chirp, taps, slots)
-    image = reduce_merge(echoes, *tables)
+    image = reduce_merge(echoes, *tables, taps)
     return jnp.transpose(image, (1, 0, 2))
 
 

time: 85.9 us -> 81.6 us (0.950)
  the two profiles are of different devices: /device:TPU:9 before, /device:TPU:17 now
where the time goes in v2:
time: 81.6 us; the launch traced here: 81.4 us
  Pallas kernels  79.9 us (98%)
  local copies, waits for them, and re-layouts  1.49 us (2%)
    pallas_call x1, Pallas kernels, reduce_merge(): pl.pallas_call(main_kernel, out_shape=jax.ShapeDtypeStruct((8, 16, 256),...  77.4 us
    pallas_call x1, Pallas kernels, prepare(): pl.pallas_call(prep_kernel, out_shape=(jax.ShapeDtypeStruct((256, 512), b...  2.46 us

profile of v2, /device:TPU:17, one launch (start us, length us, event | category | flops | bytes accessed | tf_op | source)
XLA Modules:
  0.0 81.4 jit_solution(15615292461762955501)
XLA Ops:
  0.0 2.5 %prepare.1 = (bf16[256,512]{1,0:T(8,128)(2,1)}, bf16[256,128]{1,0:T(8,128)(2,1)}, f32[2,2,128,512]{3,2,1,0:T(8,128)}) custom-call(bf16[2,128]{1,0:T(2,128)(2,1)} %chirp_ref.1, s32[3,2,8,128]{3,2,1,0:T(8,128)} %bitcast.3, s32[1,32]{1,0:T(1,128)} %slots_ref.1), custom_call_target="tpu_custom_call" | custom-call | tf_op jit(solution)/shard_map/prepare/pallas_call | solution.py:123
  2.5 77.4 %reduce_merge.1 = bf16[8,16,256]{2,1,0:T(8,128)(2,1)} custom-call(bf16[64,256,256]{2,1,0:T(8,128)(2,1)} %x_ref.1, bf16[256,512]{1,0:T(8,128)(2,1)} %get-tuple-element.8.mc_ref, bf16[256,128]{1,0:T(8,128)(2,1)} %get-tuple-element.9.a_ref, f32[2,2,128,512]{3,2,1,0:T(8,128)} %get-tuple-element.10.d0_ref, s32[3,2,8,128]{3,2,1,0:T(8,128)} %bitcast.4), custom_call_target="tpu_custom_call" | custom-call | tf_op jit(solution)/shard_map/reduce_merge/pallas_call | solution.py:557
  79.9 1.5 %copy.5 = bf16[16,8,256]{2,1,0:T(8,128)(2,1)} copy(bf16[16,8,256]{2,0,1:T(8,128)(2,1)} %bitcast.2) | data formatting | bytes 131072 | tf_op jit(solution)/shard_map/transpose | solution.py:601

commit v3 on v2

--- a/solution.py
+++ b/solution.py
@@ -67,7 +67,7 @@
     return blocks
 
 
-def prep_kernel(chirp_ref, taps_ref, slots_ref, mc_ref, a_ref, d0_ref):
+def first_tables(chirp_ref, taps_ref, slots_ref, mc_ref, a_ref, d0_ref):
     leaf = lax.axis_index("leaf")
     turn = lax.axis_index("turn")
     core = leaf % 2
@@ -118,25 +118,10 @@
         d0_ref[1, 1, :, at] = -s * sign
 
 
-def prepare(chirp, taps, slots):
-    vmem = pl.BlockSpec(memory_space=pltpu.VMEM)
-    return pl.pallas_call(
-        prep_kernel,
-        out_shape=(
-            jax.ShapeDtypeStruct((256, 512), bf16),
-            jax.ShapeDtypeStruct((256, 128), bf16),
-            jax.ShapeDtypeStruct((2, 2, BEAMS, COLS), f32),
-        ),
-        in_specs=[vmem, vmem, pl.BlockSpec(memory_space=pltpu.SMEM)],
-        out_specs=(vmem,) * 3,
-        name="prepare",
-    )(chirp, taps, slots)
-
-
 def main_kernel(
-    x_ref, mc_ref, a_ref, d0_ref, taps_ref, out_ref,
+    x_ref, chirp_ref, taps_ref, slots_ref, out_ref,
     xbuf, ebuf, u, edge, edges, xb, aoth, ay, az,
-    rby, sby, rbz, sbz, rb2, sb2, rb3, sb3, img, vout, rl, i12, d12,
+    rby, sby, rbz, sbz, rb2, sb2, rb3, sb3, img, vout, rl, i12, d12, mc_ref, a_ref, d0_ref,
     in_sem, e_sem, ex_s, ex_r, a_s, a_r, y_s, y_r, z_s, z_r, s2_s, s2_r, s3_s, s3_r, l_s, l_r,
 ):
     leaf = lax.axis_index("leaf")
@@ -177,7 +162,7 @@
         pl.semaphore_signal(barrier, inc=1, device_id={"turn": t}, device_id_type=MESH)
     for e in range(1, NLEAF):
         pl.semaphore_signal(barrier, inc=1, device_id={"leaf": (leaf + e) % NLEAF}, device_id_type=MESH)
-    pl.semaphore_wait(barrier, 4 + NLEAF - 1)
+    first_tables(chirp_ref, taps_ref, slots_ref, mc_ref, a_ref, d0_ref)
 
     def remote(src, dst, ssem, rsem, where):
         return pltpu.make_async_remote_copy(
@@ -186,7 +171,6 @@
         )
 
     a_copy = remote(a_ref, aoth, a_s, a_r, {"leaf": mate})
-    a_copy.start()
 
     def exchange(i):
         four = pl.ds(4 * chunk(i), 4)
@@ -247,10 +231,18 @@
 
         lax.fori_loop(0, 2, both, 0)
         edges[here] = edge[...]
-        exchange(i).start()
-
+
+    rby[:, 12] = jnp.zeros((2, BY, WIDE), bf16)
+    rbz[:, 14] = jnp.zeros((2, BZ, WIDE), bf16)
+    for d in range(2):
+        unsent = slice(COLS, WIDE) if d == 0 else slice(0, COLS)
+        rb2[d, 0, :, unsent] = jnp.zeros((BY, COLS), bf16)
+        rb3[d, 0, :, unsent] = jnp.zeros((BZ, COLS), bf16)
     edges[NZ] = jnp.zeros((2, SUBP, 128), f32)
     compress(0)
+    pl.semaphore_wait(barrier, 4 + NLEAF - 1)
+    a_copy.start()
+    exchange(0).start()
 
     a_copy.wait()
     for ref, low, count in ((ay, 0, BY), (az, BY, BZ)):
@@ -261,13 +253,6 @@
             ref[part * count : (part + 1) * count, 128:256] = other
             ref[(2 + part) * count : (3 + part) * count, 0:128] = mine
             ref[(2 + part) * count : (3 + part) * count, 128:256] = -other
-
-    rby[:, 12] = jnp.zeros((2, BY, WIDE), bf16)
-    rbz[:, 14] = jnp.zeros((2, BZ, WIDE), bf16)
-    for d in range(2):
-        unsent = slice(COLS, WIDE) if d == 0 else slice(0, COLS)
-        rb2[d, 0, :, unsent] = jnp.zeros((BY, COLS), bf16)
-        rb3[d, 0, :, unsent] = jnp.zeros((BZ, COLS), bf16)
 
     def partial_image(ref, low, count, tile, adds, put):
         par = tile % 2
@@ -412,6 +397,7 @@
         @pl.when(i < NZ)
         def _():
             compress(i)
+            exchange(i).start()
 
         @pl.when(i <= NZ)
         def _():
@@ -551,13 +537,13 @@
         share(e).wait_send()
 
 
-def reduce_merge(x, mc, a, d0, taps):
+def reduce_merge(x, chirp, taps, slots):
     vmem = pl.BlockSpec(memory_space=pltpu.VMEM)
     dma = pltpu.SemaphoreType.DMA
     return pl.pallas_call(
         main_kernel,
         out_shape=jax.ShapeDtypeStruct((8, 16, 256), bf16),
-        in_specs=[pl.BlockSpec(memory_space=pl.ANY)] + [vmem] * 4,
+        in_specs=[pl.BlockSpec(memory_space=pl.ANY), vmem, vmem, pl.BlockSpec(memory_space=pltpu.SMEM)],
         out_specs=vmem,
         scratch_shapes=[
             pltpu.VMEM((2, 2, SUBP, GRAN, 256), bf16),
@@ -582,6 +568,9 @@
             pltpu.VMEM((NLEAF, 16, WIDE), bf16),
             pltpu.VMEM((2, BEAMS, BEAMS), bf16),
             pltpu.VMEM((2, 2, BEAMS, COLS), f32),
+            pltpu.VMEM((256, 512), bf16),
+            pltpu.VMEM((256, 128), bf16),
+            pltpu.VMEM((2, 2, BEAMS, COLS), f32),
             dma((2, 2)), dma((2,)), dma((NZ,)), dma((NZ,)), dma, dma,
             dma((2, 12)), dma((2, 12)), dma((2, 14)), dma((2, 14)),
             dma((2, 4)), dma((2, 4)), dma((2, 2)), dma((2, 2)),
@@ -591,13 +580,12 @@
             collective_id=0, has_side_effects=True, vmem_limit_bytes=60 * 1024 * 1024
         ),
         name="reduce_merge",
-    )(x, mc, a, d0, taps)
+    )(x, chirp, taps, slots)
 
 
 def per_device(echoes, chirp, taps, slots):
     taps = jnp.transpose(taps, (0, 1, 3, 2))
-    tables = prepare(chirp, taps, slots)
-    image = reduce_merge(echoes, *tables, taps)
+    image = reduce_merge(echoes, chirp, taps, slots)
     return jnp.transpose(image, (1, 0, 2))
 
 

time: 81.6 us -> 78.1 us (0.957)
  the two profiles are of different devices: /device:TPU:17 before, /device:TPU:1 now
where the time goes in v3:
time: 78.1 us; the launch traced here: 77.9 us
  Pallas kernels  76.4 us (98%)
  local copies, waits for them, and re-layouts  1.49 us (2%)
    pallas_call x1, Pallas kernels, reduce_merge(): pl.pallas_call(main_kernel, out_shape=jax.ShapeDtypeStruct((8, 16, 256),...  76.4 us

profile of v3, /device:TPU:1, one launch (start us, length us, event | category | flops | bytes accessed | tf_op | source)
XLA Modules:
  0.0 77.9 jit_solution(3026946697524047804)
XLA Ops:
  0.0 76.4 %reduce_merge.1 = bf16[8,16,256]{2,1,0:T(8,128)(2,1)} custom-call(bf16[64,256,256]{2,1,0:T(8,128)(2,1)} %x_ref.1, bf16[2,128]{1,0:T(2,128)(2,1)} %chirp_ref.1, s32[3,2,8,128]{3,2,1,0:T(8,128)} %bitcast.3, s32[1,32]{1,0:T(1,128)} %slots_ref.1), custom_call_target="tpu_custom_call" | custom-call | tf_op jit(solution)/shard_map/reduce_merge/pallas_call | solution.py:543
  76.4 1.5 %copy.5 = bf16[16,8,256]{2,1,0:T(8,128)(2,1)} copy(bf16[16,8,256]{2,0,1:T(8,128)(2,1)} %bitcast.2) | data formatting | bytes 131072 | tf_op jit(solution)/shard_map/transpose | solution.py:589

commit v4 on v3

--- a/solution.py
+++ b/solution.py
@@ -179,27 +179,37 @@
     def granule(i, g):
         pull(i, g).wait()
         gi = 2 * chunk(i) + 1 - g
-        for hf in range(2):
-            rows = xbuf[i % 2, g, pl.ds(32 * hf, 32)].reshape(32 * GRAN, 256)
-            prod = jnp.dot(rows, mc_ref[...], preferred_element_type=f32).reshape(32, 2, 8, 512)
-            for q in range(4):
-                for e in range(2):
-                    part = prod[:, e, :, 128 * q : 128 * q + 128].reshape(256, 128)
-                    u[q, e, 256 * hf : 256 * hf + 256, :] = part
-        for b in range(GRAN):
-            half = b % 8 // 4
-            plane = 2 * (core if half == 0 else 1 - core)
-            tile = 2 * gi + b // 8
-            at = 128 * (b % 4)
+        group = SUBP // 4
+        bottom = iota((group, 8, 128), 1) == 7
+
+        def multiply(n):
+            at = pl.ds(group * n, group)
+            rows = xbuf[i % 2, g, at].reshape(group * GRAN, 256)
+            prod = jnp.dot(rows, mc_ref[...], preferred_element_type=f32).reshape(group, 2, 8, 512)
             for q in range(2):
-                own = u[q, b // 8, pl.ds(b % 8, SUBP, stride=8), :]
-                if b == GRAN - 1:
-                    nxt = edge[q]
-                else:
-                    nxt = u[2 + q, (b + 1) // 8, pl.ds((b + 1) % 8, SUBP, stride=8), :]
-                xb[tile, plane, 64 * q : 64 * q + 64, at : at + 128] = (own + nxt).astype(bf16)
-        for q in range(2):
-            edge[q] = u[2 + q, 0, pl.ds(0, SUBP, stride=8), :]
+                cols = slice(128 * q, 128 * q + 128)
+                nexts = slice(256 + 128 * q, 384 + 128 * q)
+                first, second = (pltpu.roll(prod[:, e, :, nexts], 7, 1) for e in range(2))
+                u[n, q, 0] = (prod[:, 0, :, cols] + jnp.where(bottom, second, first)).reshape(group * 8, 128)
+                third = edge[q, at]
+                u[n, q, 1] = (prod[:, 1, :, cols] + jnp.where(bottom, third, second)).reshape(group * 8, 128)
+                edge[q, at] = first
+
+        def gather(n):
+            for b in range(GRAN):
+                half = b % 8 // 4
+                plane = 2 * (core if half == 0 else 1 - core)
+                tile = 2 * gi + b // 8
+                cols = slice(128 * (b % 4), 128 * (b % 4) + 128)
+                for q in range(2):
+                    own = u[n, q, b // 8, pl.ds(b % 8, group, stride=8), :]
+                    xb[tile, plane, SUBP * q + group * n : SUBP * q + group * n + group, cols] = own.astype(bf16)
+
+        for n in range(4):
+            multiply(n)
+            if n > 0:
+                gather(n - 1)
+        gather(4 - 1)
 
     def compress(i):
         @pl.when(i + 1 < NZ)
@@ -217,11 +227,9 @@
         def _():
             pull_edge(i).wait()
             rows = ebuf[i // 2 % 2].reshape(SUBP * 8, 256)
-            prod = jnp.dot(rows, mc_ref[:, 256:512], preferred_element_type=f32)
+            prod = jnp.dot(rows, mc_ref[:, 256:512], preferred_element_type=f32).reshape(SUBP, 8, 256)
             for q in range(2):
-                u[q, 0] = prod[:, 128 * q : 128 * q + 128]
-            for q in range(2):
-                edges[(here + 1) % NZ, q] = u[q, 0, pl.ds(0, SUBP, stride=8), :]
+                edges[(here + 1) % NZ, q] = pltpu.roll(prod[:, :, 128 * q : 128 * q + 128], 7, 1)
 
         edge[...] = edges[here + 1]
 
@@ -238,7 +246,7 @@
         unsent = slice(COLS, WIDE) if d == 0 else slice(0, COLS)
         rb2[d, 0, :, unsent] = jnp.zeros((BY, COLS), bf16)
         rb3[d, 0, :, unsent] = jnp.zeros((BZ, COLS), bf16)
-    edges[NZ] = jnp.zeros((2, SUBP, 128), f32)
+    edges[NZ] = jnp.zeros((2, SUBP, 8, 128), f32)
     compress(0)
     pl.semaphore_wait(barrier, 4 + NLEAF - 1)
     a_copy.start()
@@ -418,7 +426,7 @@
 
             lax.fori_loop(0, 4, far, 0)
 
-        @pl.when((i >= 3) & (i <= NZ))
+        @pl.when((i >= 3) & (i <= 8))
         def _():
             def near(j, carry):
                 z_near(i - 2, j)
@@ -426,48 +434,52 @@
 
             lax.fori_loop(0, 4, near, 0)
 
-        @pl.when(i >= 4)
+        @pl.when((i >= 4) & (i < 12))
         def _():
             def pair(n, carry):
-                y_message(i - 4, 1, (i + n) % 2)
+                y_message(i - 4, 1, (i - 4 + n) % 2)
                 return carry
 
             lax.fori_loop(0, jnp.where(i < 8, 1, 2), pair, 0)
 
-        @pl.when(i == NZ)
+        @pl.when(i == 11)
+        def _():
+            beam = iota((BEAMS, 128), 0)
+            odd = 2 * beam + 1 - BEAMS
+            bins = iota((BEAMS, 128), 1) + 1 + COLS * core + 2 * COLS * turn
+            for level in (1, 2):
+                side = (leaf >> level) % 2
+                i12[level - 1] = interp(taps_ref[level, side])
+                rate = odd * ((2 * side - 1) * (level + 2))
+                blocks = phase_blocks(rate * bins + beam * beam * (side + 1), rate * 128, COLS // 128)
+                for b, (c, s) in enumerate(blocks):
+                    at = slice(128 * b, 128 * b + 128)
+                    d12[level - 1, 0, :, at] = c
+                    d12[level - 1, 1, :, at] = s
+
+        @pl.when(i == 7)
         def _():
             second_far()
 
-        @pl.when(i > NZ)
-        def _():
-            second_y(i - NZ)
+        @pl.when((i > 7) & (i <= 13))
+        def _():
+            second_y(i - 7)
+
+        @pl.when(i == 10)
+        def _():
+            second_z(0)
+
+        @pl.when(i == 11)
+        def _():
+            second_z(1)
+
+        @pl.when(i == 13)
+        def _():
+            second_z(2)
 
         return carry
 
-    lax.fori_loop(1, 12, main_loop, 0)
-
-    def second_loop(i, carry):
-        second_y(i)
-        return carry
-
-    beam = iota((BEAMS, 128), 0)
-    odd = 2 * beam + 1 - BEAMS
-    bins = iota((BEAMS, 128), 1) + 1 + COLS * core + 2 * COLS * turn
-    for level in (1, 2):
-        side = (leaf >> level) % 2
-        i12[level - 1] = interp(taps_ref[level, side])
-        rate = odd * ((2 * side - 1) * (level + 2))
-        blocks = phase_blocks(rate * bins + beam * beam * (side + 1), rate * 128, COLS // 128)
-        for b, (c, s) in enumerate(blocks):
-            at = slice(128 * b, 128 * b + 128)
-            d12[level - 1, 0, :, at] = c
-            d12[level - 1, 1, :, at] = s
-
-    second_z(0)
-    lax.fori_loop(4, 5, second_loop, 0)
-    second_z(1)
-    second_z(2)
-    lax.fori_loop(5, 7, second_loop, 0)
+    lax.fori_loop(1, 14, main_loop, 0)
     second_z(3)
     adds = wait_y(7)
     for d in range(2):
@@ -548,9 +560,9 @@
         scratch_shapes=[
             pltpu.VMEM((2, 2, SUBP, GRAN, 256), bf16),
             pltpu.VMEM((2, SUBP, 8, 256), bf16),
-            pltpu.VMEM((4, 2, SUBP * 8, 128), f32),
-            pltpu.VMEM((2, SUBP, 128), f32),
-            pltpu.VMEM((NZ + 1, 2, SUBP, 128), f32),
+            pltpu.VMEM((4, 2, 2, SUBP * 8 // 4, 128), f32),
+            pltpu.VMEM((2, SUBP, 8, 128), f32),
+            pltpu.VMEM((NZ + 1, 2, SUBP, 8, 128), f32),
             pltpu.VMEM((TILES, 3, 128, COLS), bf16),
             pltpu.VMEM((256, 128), bf16),
             pltpu.VMEM((4 * BY, 256), bf16),

time: 78.1 us -> 75.3 us (0.964)
  Pallas kernels: 76.4 us -> 73.6 us
    pallas_call x1, Pallas kernels: 76.4 us -> 73.6 us  [reduce_merge(): pl.pallas_call(main_kernel, out_shape=jax.ShapeDtypeStruct((8, 16, 256),...]
where the time goes in v4:
time: 75.3 us; the launch traced here: 75.1 us
  Pallas kernels  73.6 us (98%)
  local copies, waits for them, and re-layouts  1.49 us (2%)
    pallas_call x1, Pallas kernels, reduce_merge(): pl.pallas_call(main_kernel, out_shape=jax.ShapeDtypeStruct((8, 16, 256),...  73.6 us

profile of v4, /device:TPU:1, one launch (start us, length us, event | category | flops | bytes accessed | tf_op | source)
XLA Modules:
  0.0 75.1 jit_solution(4270369960537770269)
XLA Ops:
  0.0 73.6 %reduce_merge.1 = bf16[8,16,256]{2,1,0:T(8,128)(2,1)} custom-call(bf16[64,256,256]{2,1,0:T(8,128)(2,1)} %x_ref.1, bf16[2,128]{1,0:T(2,128)(2,1)} %chirp_ref.1, s32[3,2,8,128]{3,2,1,0:T(8,128)} %bitcast.3, s32[1,32]{1,0:T(1,128)} %slots_ref.1), custom_call_target="tpu_custom_call" | custom-call | tf_op jit(solution)/shard_map/reduce_merge/pallas_call | solution.py:555
  73.6 1.5 %copy.5 = bf16[16,8,256]{2,1,0:T(8,128)(2,1)} copy(bf16[16,8,256]{2,0,1:T(8,128)(2,1)} %bitcast.2) | data formatting | bytes 131072 | tf_op jit(solution)/shard_map/transpose | solution.py:601

commit v5 on v4

--- a/solution.py
+++ b/solution.py
@@ -416,7 +416,7 @@
                 y_message(c, near, (c + near) % 2)
                 return carry
 
-            lax.fori_loop(0, jnp.where(c < 4, 2, 1), pair, 0)
+            lax.fori_loop(0, jnp.where(c < 2, 2, 1), pair, 0)
 
         @pl.when(i == 1)
         def _():
@@ -426,10 +426,10 @@
 
             lax.fori_loop(0, 4, far, 0)
 
-        @pl.when((i >= 3) & (i <= 8))
+        @pl.when((i >= 4) & (i <= 9))
         def _():
             def near(j, carry):
-                z_near(i - 2, j)
+                z_near(i - 3, j)
                 return carry
 
             lax.fori_loop(0, 4, near, 0)
@@ -440,7 +440,7 @@
                 y_message(i - 4, 1, (i - 4 + n) % 2)
                 return carry
 
-            lax.fori_loop(0, jnp.where(i < 8, 1, 2), pair, 0)
+            lax.fori_loop(0, jnp.where(i < 6, 1, 2), pair, 0)
 
         @pl.when(i == 11)
         def _():
@@ -457,13 +457,13 @@
                     d12[level - 1, 0, :, at] = c
                     d12[level - 1, 1, :, at] = s
 
-        @pl.when(i == 7)
+        @pl.when(i == 6)
         def _():
             second_far()
 
-        @pl.when((i > 7) & (i <= 13))
-        def _():
-            second_y(i - 7)
+        @pl.when((i > 6) & (i <= 12))
+        def _():
+            second_y(i - 6)
 
         @pl.when(i == 10)
         def _():
@@ -511,6 +511,30 @@
     for e in range(1, NLEAF):
         share(e).start()
     rl[leaf] = vout[pl.ds(pl.multiple_of(16 * leaf, 16), 16)]
+    def sent_y(k, carry):
+        for d in range(2):
+            y_copy(d, k).wait_send()
+        return carry
+
+    def sent_z(k, carry):
+        for d in range(2):
+            z_copy(d, k).wait_send()
+        return carry
+
+    def sent_mate(i, carry):
+        exchange(i).wait_send()
+        return carry
+
+    lax.fori_loop(0, NZ, sent_mate, 0)
+    lax.fori_loop(0, 12, sent_y, 0)
+    lax.fori_loop(0, 14, sent_z, 0)
+    for d in range(2):
+        far2(d).wait_send()
+        far3(d).wait_send()
+        near3(d, 1).wait_send()
+        for k in range(1, 4):
+            near2(d, k).wait_send()
+
     for e in range(1, NLEAF):
         shared(e).wait_recv()
     for side in range(2):
@@ -522,29 +546,6 @@
             out_ref[4 * side + b, :, 0:128] = total[:, 128 * b : 128 * b + 128]
             out_ref[4 * side + b, :, 128:256] = total[:, COLS + 128 * b : COLS + 128 * b + 128]
 
-    def sent_y(k, carry):
-        for d in range(2):
-            y_copy(d, k).wait_send()
-        return carry
-
-    def sent_z(k, carry):
-        for d in range(2):
-            z_copy(d, k).wait_send()
-        return carry
-
-    def sent_mate(i, carry):
-        exchange(i).wait_send()
-        return carry
-
-    lax.fori_loop(0, NZ, sent_mate, 0)
-    lax.fori_loop(0, 12, sent_y, 0)
-    lax.fori_loop(0, 14, sent_z, 0)
-    for d in range(2):
-        far2(d).wait_send()
-        far3(d).wait_send()
-        near3(d, 1).wait_send()
-        for k in range(1, 4):
-            near2(d, k).wait_send()
     for e in range(1, NLEAF):
         share(e).wait_send()
 

time: 75.3 us -> 73.4 us (0.975)
  Pallas kernels: 73.6 us -> 71.7 us
    pallas_call x1, Pallas kernels: 73.6 us -> 71.7 us  [reduce_merge(): pl.pallas_call(main_kernel, out_shape=jax.ShapeDtypeStruct((8, 16, 256),...]
where the time goes in v5:
time: 73.4 us; the launch traced here: 73.2 us
  Pallas kernels  71.7 us (98%)
  local copies, waits for them, and re-layouts  1.49 us (2%)
    pallas_call x1, Pallas kernels, reduce_merge(): pl.pallas_call(main_kernel, out_shape=jax.ShapeDtypeStruct((8, 16, 256),...  71.7 us
    transpose x1, local copies, waits for them, and re-layouts, per_device(): return jnp.transpose(image, (1, 0, 2))  1.49 us

profile of v5, /device:TPU:1, one launch (start us, length us, event | category | flops | bytes accessed | tf_op | source)
XLA Modules:
  0.0 73.2 jit_solution(10055881587996165652)
XLA Ops:
  0.0 71.7 %reduce_merge.1 = bf16[8,16,256]{2,1,0:T(8,128)(2,1)} custom-call(bf16[64,256,256]{2,1,0:T(8,128)(2,1)} %x_ref.1, bf16[2,128]{1,0:T(2,128)(2,1)} %chirp_ref.1, s32[3,2,8,128]{3,2,1,0:T(8,128)} %bitcast.3, s32[1,32]{1,0:T(1,128)} %slots_ref.1), custom_call_target="tpu_custom_call" | custom-call | tf_op jit(solution)/shard_map/reduce_merge/pallas_call | solution.py:556
  71.8 1.5 %copy.5 = bf16[16,8,256]{2,1,0:T(8,128)(2,1)} copy(bf16[16,8,256]{2,0,1:T(8,128)(2,1)} %bitcast.2) | data formatting | bytes 131072 | tf_op jit(solution)/shard_map/transpose | solution.py:602

commit v6 on v5

--- a/solution.py
+++ b/solution.py
@@ -442,7 +442,27 @@
 
             lax.fori_loop(0, jnp.where(i < 6, 1, 2), pair, 0)
 
+        @pl.when(i == 6)
+        def _():
+            second_far()
+
+        @pl.when((i > 6) & (i <= 12))
+        def _():
+            second_y(i - 6)
+
+        @pl.when(i == 10)
+        def _():
+            second_z(0)
+
         @pl.when(i == 11)
+        def _():
+            second_z(1)
+
+        @pl.when(i == 13)
+        def _():
+            second_z(2)
+
+        @pl.when(i == 13)
         def _():
             beam = iota((BEAMS, 128), 0)
             odd = 2 * beam + 1 - BEAMS
@@ -456,26 +476,6 @@
                     at = slice(128 * b, 128 * b + 128)
                     d12[level - 1, 0, :, at] = c
                     d12[level - 1, 1, :, at] = s
-
-        @pl.when(i == 6)
-        def _():
-            second_far()
-
-        @pl.when((i > 6) & (i <= 12))
-        def _():
-            second_y(i - 6)
-
-        @pl.when(i == 10)
-        def _():
-            second_z(0)
-
-        @pl.when(i == 11)
-        def _():
-            second_z(1)
-
-        @pl.when(i == 13)
-        def _():
-            second_z(2)
 
         return carry
 

time: 73.4 us -> 73.4 us (level)
  no operation moved by 1% of the time
where the time goes in v6:
time: 73.4 us; the launch traced here: 73.2 us
  Pallas kernels  71.7 us (98%)
  local copies, waits for them, and re-layouts  1.49 us (2%)
    pallas_call x1, Pallas kernels, reduce_merge(): pl.pallas_call(main_kernel, out_shape=jax.ShapeDtypeStruct((8, 16, 256),...  71.7 us
    transpose x1, local copies, waits for them, and re-layouts, per_device(): return jnp.transpose(image, (1, 0, 2))  1.49 us

profile of v6, /device:TPU:1, one launch (start us, length us, event | category | flops | bytes accessed | tf_op | source)
XLA Modules:
  0.0 73.2 jit_solution(14614262336906302164)
XLA Ops:
  0.0 71.7 %reduce_merge.1 = bf16[8,16,256]{2,1,0:T(8,128)(2,1)} custom-call(bf16[64,256,256]{2,1,0:T(8,128)(2,1)} %x_ref.1, bf16[2,128]{1,0:T(2,128)(2,1)} %chirp_ref.1, s32[3,2,8,128]{3,2,1,0:T(8,128)} %bitcast.3, s32[1,32]{1,0:T(1,128)} %slots_ref.1), custom_call_target="tpu_custom_call" | custom-call | tf_op jit(solution)/shard_map/reduce_merge/pallas_call | solution.py:556
  71.7 1.5 %copy.5 = bf16[16,8,256]{2,1,0:T(8,128)(2,1)} copy(bf16[16,8,256]{2,0,1:T(8,128)(2,1)} %bitcast.2) | data formatting | bytes 131072 | tf_op jit(solution)/shard_map/transpose | solution.py:602
